TPU v7x, 256 devices: a whole 4x4x8 slice. The times are simulated.
256 devices in a mesh: frame: 32 (over z_hi, y, core), head: 8 (over z_lo, x).
Axes of the slice: x: 4, y: 4, z: 8 (z_hi: 4, z_lo: 2; z = z_hi * 2 + z_lo), core: 2. Of those that a mesh axis runs over, the one named last changes fastest.
Arguments:
- tokens: bfloat16 [8192, 3072], P('frame'), may hold values from -6 to 6
- w_qkv: bfloat16 [3, 3072, 3072], P(None, None, 'head'), may hold values from -0.109375 to 0.109375
- norm_gains: float32 [2, 3072], P(None, 'head'), may hold values from 0.8 to 2.5
- w_out: bfloat16 [3072, 3072], P('head'), may hold values from -0.15625 to 0.15625
- near_mask: int32 [64, 4], P('frame'), may hold values 0 or 1
- far_pattern: int32 [64, 64], P('frame'), may hold values from 0 to 1, as said below
- window: int32 [32], replicated, may hold values from 1 to 256, as said below
Outputs:
- layer_out: bfloat16 [8192, 3072], P('frame', 'head')
- checksum: float32 [8192], P('frame')
Inputs may be any that keep to these rules, and one draw needn't show every extreme that they name: `far_pattern`: 0 or 1; entries whose two blocks lie in slabs less than two apart are never read. Entry d is the window for slabs d apart; entry 0 is 256.
All inputs are finite; a program needn't handle non-finite values. No bound on the sum of `near_mask` on one device may be relied on, other than what follows from the above.
Results may differ from a plain program's by a relative error of at most 0.015.
Values may be sent and summed in bfloat16 or wider, within the bound.
A program may use at most 128 MiB of HBM per device.

v0:
```python
import jax
import jax.numpy as jnp
from jax import lax
from jax.sharding import PartitionSpec as P

D = 3072
HD = 128
BLK = 128


def with_halo(cells, sides, width):
    for axis, dim in sides:
        count = lax.axis_size(axis)
        ends = count - 1
        head = lax.slice_in_dim(cells, 0, width, axis=dim)
        tail = lax.slice_in_dim(cells, cells.shape[dim] - width, cells.shape[dim], axis=dim)
        cells = jnp.concatenate(
            [
                lax.ppermute(tail, axis, [(i, (i + 1) % count) for i in range(ends)]),
                cells,
                lax.ppermute(head, axis, [((i + 1) % count, i) for i in range(ends)]),
            ],
            axis=dim,
        )
    return cells


def normed_heads(values, gain_row):
    shaped = values.reshape(values.shape[0], -1, HD)
    factor = lax.rsqrt(jnp.mean(shaped * shaped, axis=-1, keepdims=True) + 1e-06)
    return shaped * factor * gain_row.reshape(-1, HD)


def lookup_columns(table_int, columns, table_width):
    onehot = (jnp.arange(table_width, dtype=jnp.int32)[:, None] == columns[None, :]).astype(
        jnp.float32
    )
    return jnp.dot(table_int.astype(jnp.float32), onehot)


def attend(totals, key_part, value_part, first_row, context, which_keys):
    queries, near_mask, far_pattern, window, frame_id, slab_rows, n_frame = context
    numer, denom = totals
    key_span = key_part.shape[0]
    n_blocks = near_mask.shape[0]
    key_index = first_row + jnp.arange(key_span, dtype=jnp.int32)
    key_slab = key_index // slab_rows
    key_pos = key_index % slab_rows
    distance = jnp.abs(key_slab - frame_id)
    far_sel = lookup_columns(far_pattern, key_index // BLK, far_pattern.shape[1])
    key_side = jnp.where(key_slab < frame_id, 0, 1)
    near_sel = lookup_columns(near_mask, key_side * n_blocks + key_pos // BLK, 2 * n_blocks)
    if which_keys == "near":
        chosen = jnp.where(distance == 0, 1.0, jnp.where(distance == 1, near_sel, 0.0))
    else:
        chosen = jnp.where(distance >= 2, far_sel, 0.0)
    chosen = jnp.broadcast_to(chosen[:, None, :], (n_blocks, BLK, key_span)).reshape(
        slab_rows, key_span
    )
    inside = (key_index >= 0) & (key_index < slab_rows * n_frame)
    slab_steps = jnp.arange(n_frame, dtype=jnp.int32)
    key_limit = jnp.sum(
        jnp.where(slab_steps[:, None] == distance[None, :], window[:, None], 0), axis=0
    )
    position = jnp.arange(slab_rows, dtype=jnp.int32)
    allowed = (
        (chosen > 0.5)
        & inside[None, :]
        & (jnp.abs(position[:, None] - key_pos[None, :]) < key_limit[None, :])
    )
    key_heads = key_part.reshape(key_span, -1, HD)
    value_heads = value_part.reshape(key_span, -1, HD)
    scores = jnp.einsum("qhd,khd->hqk", queries, key_heads, preferred_element_type=jnp.float32)
    weights = jnp.where(allowed[None], jnp.exp(scores), 0.0)
    numer = numer + jnp.einsum(
        "hqk,khd->qhd",
        weights.astype(jnp.bfloat16),
        value_heads,
        preferred_element_type=jnp.float32,
    )
    denom = denom + jnp.sum(weights, axis=-1)
    return (numer, denom)


def per_device(tokens, w_qkv, norm_gains, w_out, near_mask, far_pattern, window):
    slab_rows = tokens.shape[0]
    frame_id = lax.axis_index("frame")
    n_frame = lax.axis_size("frame")
    query = jnp.dot(tokens, w_qkv[0], preferred_element_type=jnp.float32)
    key_full = jnp.dot(tokens, w_qkv[1], preferred_element_type=jnp.float32)
    value_full = jnp.dot(tokens, w_qkv[2], preferred_element_type=jnp.float32)
    queries = (normed_heads(query, norm_gains[0]) * HD ** (-0.5)).astype(jnp.bfloat16)
    keys_flat = normed_heads(key_full, norm_gains[1]).astype(jnp.bfloat16).reshape(slab_rows, -1)
    values_flat = value_full.astype(jnp.bfloat16)
    head_count = queries.shape[1]
    context = (queries, near_mask, far_pattern, window, frame_id, slab_rows, n_frame)
    start_totals = (
        jnp.zeros((slab_rows, head_count, HD), jnp.float32),
        jnp.zeros((head_count, slab_rows), jnp.float32),
    )
    stacked = jnp.stack([keys_flat, values_flat])
    widened = with_halo(stacked, (("frame", 1),), slab_rows)
    totals = attend(
        start_totals, widened[0], widened[1], (frame_id - 1) * slab_rows, context, "near"
    )
    totals = attend(
        totals,
        lax.all_gather(keys_flat, "frame", axis=0, tiled=True),
        lax.all_gather(values_flat, "frame", axis=0, tiled=True),
        jnp.int32(0),
        context,
        "far",
    )
    numer, denom = totals
    attended = (numer / denom.T[:, :, None]).reshape(slab_rows, -1).astype(jnp.bfloat16)
    full_cols = lax.psum_scatter(
        lax.dot_general(
            w_out, attended, (((0,), (1,)), ((), ())), preferred_element_type=jnp.float32
        ).astype(jnp.bfloat16),
        "head",
        scatter_dimension=0,
        tiled=True,
    ).astype(jnp.float32)
    full_rows = full_cols.T
    layer_out = full_rows.astype(jnp.bfloat16)
    checksum = lax.psum(jnp.sum(full_rows, axis=1) * D ** (-0.5), "head")
    return (layer_out, checksum)


def solution(mesh):
    in_specs = (
        P("frame", None),
        P(None, None, "head"),
        P(None, "head"),
        P("head", None),
        P("frame", None),
        P("frame", None),
        P(),
    )
    out_specs = (P("frame", "head"), P("frame"))
    return jax.shard_map(
        per_device, mesh=mesh, in_specs=in_specs, out_specs=out_specs, check_vma=False
    )
```

profile of v0, /device:TPU:8, one launch (start us, length us, event | category | flops | bytes accessed | tf_op | source)
XLA Modules:
  0.0 266.5 jit_solution(1134250349421031782)
XLA Ops:
  7.2 0.0 copy-start
  7.2 0.0 all-gather.5.cloned.1.call-start
  7.2 5.1 %slice_bitcast_fusion = (bf16[384,3072]{0,1:T(8,128)(2,1)}, bf16[384,3072]{0,1:T(8,128)(2,1)}) fusion(bf16[3,3072,384]{2,1,0:T(8,128)(2,1)} %param.8), kind=kLoop, calls=%fused_computation.17 | loop fusion | bytes 9437184 | tf_op jit(solution)/shard_map/dot_general | solution.py:89
  12.4 4.3 %copy.37 = bf16[384,3072]{1,0:T(8,128)(2,1)} copy(bf16[384,3072]{0,1:T(8,128)(2,1)} %get-tuple-element.5) | data formatting | bytes 4718592 | tf_op jit(solution)/shard_map/dot_general | solution.py:90
  16.7 3.0 %multiply_reduce_fusion.1 = (f32[256,3]{0,1:T(4,128)S(1)}, f32[256,3,128]{0,2,1:T(8,128)S(1)}) fusion(bf16[3,128,3072]{2,1,0:T(8,128)(2,1)} %bitcast.69, bf16[256,3072]{1,0:T(8,128)(2,1)} %param.7), kind=kOutput, calls=%fused_computation.50 | convolution fusion | flops 604175616 | bytes 4328448 | tf_op jit(solution)/shard_map/dot_general | solution.py:90
  19.6 0.8 multiply_convert_fusion.1
  20.4 0.0 all-gather.5.cloned.1.call-update
  20.5 0.0 copy-start.3
  20.5 0.0 all-gather.3.cloned.1.call-start
  20.5 3.8 %fusion.27 = bf16[256,384]{1,0:T(8,128)(2,1)} fusion(bf16[256,3072]{1,0:T(8,128)(2,1)} %param.7, bf16[3,3072,384]{2,1,0:T(8,128)(2,1)} %param.8), kind=kOutput, calls=%fused_computation.34 | convolution fusion | flops 604078080 | bytes 4128768 | tf_op jit(solution)/shard_map/dot_general | solution.py:91
  24.4 0.0 all-gather.3.cloned.1.call-update
  24.4 0.0 reduce-scatter.4.cloned.1.call-start
  24.4 0.2 copy.38
  24.6 1.7 pad_maximum_fusion.1
  26.3 1.9 collective-permute-start.1
  28.3 2.6 collective-permute-start
  30.9 0.0 copy-start.9
  30.9 0.0 copy-start.10
  30.9 4.3 %copy.40 = bf16[384,3072]{1,0:T(8,128)(2,1)} copy(bf16[384,3072]{0,1:T(8,128)(2,1)} %get-tuple-element.4) | data formatting | bytes 4718592 | tf_op jit(solution)/shard_map/dot_general | solution.py:89
  35.3 0.2 select_reduce_fusion
  35.5 0.4 fusion.7
  36.0 3.8 %fusion.8 = pred[256,8192]{1,0:T(8,128)(4,1)} fusion(s32[8192]{0:T(1024)S(1)} %select_reduce_fusion, s32[8192]{0:T(1024)S(1)} %fusion.35, pred[8192]{0:T(1024)(128)(4,1)S(1)} %iota_compare_fusion.4, pred[2,8192]{1,0:T(4,128)(4,1)S(1)} %fusion.7), kind=kLoop, calls=%fused_computation.10 | loop fusion | flops 10485760 | bytes 2187264 | tf_op jit(solution)/shard_map/and | solution.py:67
  39.8 0.1 select_reduce_fusion.1
  39.9 0.1 fusion.32
  40.1 0.9 fusion.34
  41.0 3.0 %multiply_reduce_fusion = (f32[256,3]{0,1:T(4,128)S(1)}, f32[256,3,128]{0,2,1:T(8,128)}) fusion(bf16[3,128,3072]{2,1,0:T(8,128)(2,1)S(1)} %bitcast.68, bf16[256,3072]{1,0:T(8,128)(2,1)} %param.7), kind=kOutput, calls=%fused_computation.48 | convolution fusion | flops 604175616 | bytes 4328448 | tf_op jit(solution)/shard_map/dot_general | solution.py:89
  44.0 0.0 collective-permute-done.1
  44.1 0.0 collective-permute-done
  44.1 0.1 pad_maximum_fusion
  44.2 0.1 fusion.66
  44.3 1.1 copy.39
  45.4 0.3 copy.41
  45.7 0.0 copy-start.7
  45.7 3.2 %fusion.13 = (f32[3,256]{1,0:T(4,128)S(1)}, f32[3,256,768]{2,1,0:T(8,128)}) fusion(pred[256,768]{1,0:T(8,128)(4,1)} %fusion.34, bf16[768,3,128]{0,2,1:T(8,128)(2,1)S(1)} %bitcast.70, f32[256,3,128]{0,2,1:T(8,128)} %get-tuple-element.11, f32[3,128]{1,0:T(4,128)S(1)} %bitcast.78, f32[256,3]{0,1:T(4,128)S(1)} %add_rsqrt_fusion), kind=kOutput, calls=%fused_computation.21 | convolution fusion | flops 152567040 | bytes 3546624 | tf_op jit(solution)/shard_map/qhd,khd->hqk/dot_general | solution.py:73
  48.9 50.5 %all-gather.5.cloned.1.call-done = bf16[8192,384]{0,1:T(8,128)(2,1)} async-done(((bf16[256,384]{0,1:T(8,128)(2,1)}), bf16[8192,384]{0,1:T(8,128)(2,1)}) %all-gather.5.cloned.1.call-update) | async-done | bytes 6291472 | tf_op jit(solution)/shard_map/all_gather | solution.py:108
  99.4 14.9 %fusion = (f32[3,256]{1,0:T(4,128)S(1)}, f32[3,256,8192]{2,1,0:T(8,128)}) fusion(pred[256,8192]{1,0:T(8,128)(4,1)} %fusion.8, bf16[8192,3,128]{0,2,1:T(8,128)(2,1)} %bitcast.81, f32[256,3,128]{0,2,1:T(8,128)S(1)} %copy-done.7, f32[3,128]{1,0:T(4,128)S(1)} %bitcast.79, f32[256,3]{0,1:T(4,128)S(1)} %add_rsqrt_fusion), kind=kOutput, calls=%fused_computation.1 | convolution fusion | flops 1623588096 | bytes 33955328 | tf_op jit(solution)/shard_map/qhd,khd->hqk/dot_general | solution.py:73
  114.3 56.0 %all-gather.3.cloned.1.call-done = bf16[8192,384]{1,0:T(8,128)(2,1)} async-done(((bf16[256,384]{1,0:T(8,128)(2,1)}), bf16[8192,384]{1,0:T(8,128)(2,1)}) %all-gather.3.cloned.1.call-update) | async-done | bytes 6291472 | tf_op jit(solution)/shard_map/all_gather | solution.py:109
  170.3 8.5 %copy.44 = bf16[8192,384]{0,1:T(8,128)(2,1)} copy(bf16[8192,384]{1,0:T(8,128)(2,1)} %all-gather.3.cloned.1.call-done) | data formatting | bytes 12582912 | tf_op jit(solution)/shard_map/all_gather | solution.py:109
  178.8 13.7 %fusion.2 = f32[3,128,256]{2,1,0:T(8,128)} fusion(bf16[8192,3,128]{0,2,1:T(8,128)(2,1)} %bitcast.67, f32[3,256,8192]{2,1,0:T(8,128)} %get-tuple-element.15, pred[256,8192]{1,0:T(8,128)(4,1)} %fusion.8), kind=kOutput, calls=%fused_computation.3 | convolution fusion | flops 1623195648 | bytes 33947648 | tf_op jit(solution)/shard_map/hqk,khd->qhd/dot_general | solution.py:75
  192.5 2.3 fusion.24
  194.8 2.2 fusion.9
  196.9 2.6 copy.51
  199.5 0.0 reduce-scatter.4.cloned.1.call-update
  199.6 41.9 %reduce-scatter.4.cloned.1.call-done = bf16[384,256]{1,0:T(8,128)(2,1)} async-done(((bf16[3072,256]{1,0:T(8,128)(2,1)}), bf16[384,256]{1,0:T(8,128)(2,1)}) %reduce-scatter.4.cloned.1.call-update) | async-done | bytes 196624
  241.4 1.1 copy.52
  242.5 0.0 copy-start.5
  242.5 0.1 convert_reduce_fusion
  242.7 17.3 %psum.7 = f32[256]{0:T(256)} all-reduce(f32[256]{0:T(256)S(1)} %broadcast_multiply_fusion), channel_id=1, replica_groups=mesh['frame'=32,'head'=8] {'head'}, use_global_device_ids=true, to_apply=%region_8.9 | all-reduce | flops 256 | bytes 2048 | tf_op jit(solution)/shard_map/psum | solution.py:126
  (32 shorter events, 0.2 us)
Async XLA Ops:
  7.2 187.6 %copy-start = (bf16[384,3072]{1,0:T(8,128)(2,1)S(1)}, bf16[384,3072]{1,0:T(8,128)(2,1)}, u32[]{:S(2)}) copy-start(bf16[384,3072]{1,0:T(8,128)(2,1)} %param.10) | copy-start | bytes 7077892
  7.2 92.2 %all-gather.5.cloned.1.call-start = ((), (), s32[]{:S(2)}) async-start(), calls=%async_computation.2 | async-start | bytes 6488064 | tf_op jit(solution)/shard_map/all_gather | solution.py:108
  12.3 4.3 %copy-start.8 = (f32[2,384]{1,0:T(2,128)S(1)}, f32[2,384]{1,0:T(2,128)}, u32[]{:S(2)}) copy-start(f32[2,384]{1,0:T(2,128)} %param.9) | copy-start | bytes 9220
  20.5 4.0 %copy-start.3 = (bf16[256,3,128]{0,2,1:T(8,128)(2,1)S(1)}, bf16[256,3,128]{0,2,1:T(8,128)(2,1)}, u32[]{:S(2)}) copy-start(bf16[256,3,128]{0,2,1:T(8,128)(2,1)} %multiply_convert_fusion.1) | copy-start | bytes 589828
  20.5 149.8 %all-gather.3.cloned.1.call-start = ((), (), s32[]{:S(2)}) async-start(), calls=%async_computation.1 | async-start | bytes 6488064 | tf_op jit(solution)/shard_map/all_gather | solution.py:109
  24.4 217.1 %reduce-scatter.4.cloned.1.call-start = ((), (), s32[]{:S(2)}) async-start(), calls=%async_computation.3 | async-start | bytes 1769472
  26.3 17.7 %collective-permute-start.1 = (bf16[2,256,384]{2,1,0:T(8,128)(2,1)}, bf16[2,256,384]{2,1,0:T(8,128)(2,1)S(1)}, u32[]{:S(2)}, u32[]{:S(2)}) collective-permute-start(bf16[2,256,384]{2,1,0:T(8,128)(2,1)} %pad_maximum_fusion.1), channel_id=1, source_target_pairs={{8,0},{16,8},{24,16},{32,24},{40,32},{48,40},{56,48},{64,56},{72,6... | collective-permute-start | bytes 1179656 | tf_op jit(solution)/shard_map/ppermute | solution.py:21
  28.3 15.8 %collective-permute-start = (bf16[2,256,384]{2,1,0:T(8,128)(2,1)}, bf16[2,256,384]{2,1,0:T(8,128)(2,1)S(1)}, u32[]{:S(2)}, u32[]{:S(2)}) collective-permute-start(bf16[2,256,384]{2,1,0:T(8,128)(2,1)} %pad_maximum_fusion.1), channel_id=1, source_target_pairs={{0,8},{8,16},{16,24},{24,32},{32,40},{40,48},{48,56},{56,64},{64,7... | collective-permute-start | bytes 1179656 | tf_op jit(solution)/shard_map/ppermute | solution.py:19
  30.9 4.4 %copy-start.9 = (s32[32]{0:T(128)S(1)}, s32[32]{0:T(128)}, u32[]{:S(2)}) copy-start(s32[32]{0:T(128)} %param.13) | copy-start | bytes 388
  30.9 4.6 %copy-start.10 = (s32[2,64]{1,0:T(2,128)S(1)}, s32[2,64]{1,0:T(2,128)}, u32[]{:S(2)}) copy-start(s32[2,64]{1,0:T(2,128)} %param.12) | copy-start | bytes 1540
  35.2 4.8 %copy-start.11 = (s32[2,4]{1,0:T(2,128)S(1)}, s32[2,4]{1,0:T(2,128)}, u32[]{:S(2)}) copy-start(s32[2,4]{1,0:T(2,128)} %param.11) | copy-start | bytes 100
  35.2 5.8 %copy-start.1 = (bf16[384,3072]{1,0:T(8,128)(2,1)S(1)}, bf16[384,3072]{1,0:T(8,128)(2,1)}, u32[]{:S(2)}) copy-start(bf16[384,3072]{1,0:T(8,128)(2,1)} %copy.40) | copy-start | bytes 7077892
  41.0 3.1 %copy-start.2 = (bf16[256,384]{1,0:T(8,128)(2,1)S(1)}, bf16[256,384]{1,0:T(8,128)(2,1)}, u32[]{:S(2)}) copy-start(bf16[256,384]{1,0:T(8,128)(2,1)} %fusion.27) | copy-start | bytes 589828
  45.7 53.7 %copy-start.7 = (f32[256,3,128]{0,2,1:T(8,128)S(1)}, f32[256,3,128]{0,2,1:T(8,128)}, u32[]{:S(2)}) copy-start(f32[256,3,128]{0,2,1:T(8,128)} %get-tuple-element.11) | copy-start | bytes 1179652
  178.8 13.7 %copy-start.4 = (pred[256,768]{1,0:T(8,128)(4,1)S(1)}, pred[256,768]{1,0:T(8,128)(4,1)}, u32[]{:S(2)}) copy-start(pred[256,768]{1,0:T(8,128)(4,1)} %fusion.34) | copy-start | bytes 589828
  178.8 13.7 %copy-start.6 = (bf16[1,768,384]{1,2,0:T(8,128)(2,1)S(1)}, bf16[1,768,384]{1,2,0:T(8,128)(2,1)}, u32[]{:S(2)}) copy-start(bf16[1,768,384]{1,2,0:T(8,128)(2,1)} %copy.39) | copy-start | bytes 1769476
  242.5 17.4 %copy-start.5 = (bf16[384,256]{0,1:T(8,128)(2,1)}, bf16[384,256]{0,1:T(8,128)(2,1)S(1)}, u32[]{:S(2)}) copy-start(bf16[384,256]{0,1:T(8,128)(2,1)S(1)} %copy.52) | copy-start | bytes 589828
Sparse Core Ops, SparseCore 0:
  20.6 78.7 all-gather.4
  102.5 67.7 all-gather.2
  199.7 41.7 reduce-scatter.3
where the time goes:
time: 267 us; the launch traced here: 266 us
  waiting for transfers between devices  148 us (55%)
  matrix products  46.6 us (17%)
  local copies, waits for them, and re-layouts  27.6 us (10%)
  blocking collectives  17.3 us (6%)
  between operations  14 us (5%)
  other arithmetic  7.97 us (3%)
  starting transfers between devices  4.62 us (2%)
    all_gather x1, waiting for transfers between devices, per_device(): lax.all_gather(values_flat, 'frame', axis=0, tiled=True)  56 us
    all_gather x1, waiting for transfers between devices, per_device(): lax.all_gather(keys_flat, 'frame', axis=0, tiled=True)  50.5 us
    unnamed x4, waiting for transfers between devices  41.9 us
    dot_general x2, matrix products, attend(): jnp.einsum('qhd,khd->hqk', queries, key_heads, preferred_element_type=jnp...  18.1 us
    psum x1, blocking collectives, per_device(): checksum = lax.psum(jnp.sum(full_rows, axis=1) * D ** (-0.5), 'head')  17.3 us
    dot_general x2, matrix products, attend(): jnp.einsum('hqk,khd->qhd', weights.astype(jnp.bfloat16), value_heads, pre...  15.9 us
    dot_general x2, local copies, waits for them, and re-layouts, per_device(): query = jnp.dot(tokens, w_qkv[0], preferred_element_type=jnp.float32)  9.4 us
    all_gather x1, local copies, waits for them, and re-layouts, per_device(): lax.all_gather(values_flat, 'frame', axis=0, tiled=True)  8.53 us
  transfers between devices with their start and end apart: 5, of which 3 were waited for; matrix products, arithmetic and copies ran while one was open for 14% of the time, Pallas kernels for 0%

commit v1 on v0

--- a/solution.py
+++ b/solution.py
@@ -6,6 +6,11 @@
 D = 3072
 HD = 128
 BLK = 128
+
+
+def all_by_exchange(shard, axis, dim):
+    repeated = jnp.stack([shard] * lax.axis_size(axis))
+    return jnp.concatenate(lax.all_to_all(repeated, axis, 0, 0), axis=dim)
 
 
 def with_halo(cells, sides, width):
@@ -106,7 +111,7 @@
     totals = attend(
         totals,
         lax.all_gather(keys_flat, "frame", axis=0, tiled=True),
-        lax.all_gather(values_flat, "frame", axis=0, tiled=True),
+        all_by_exchange(values_flat, "frame", 0),
         jnp.int32(0),
         context,
         "far",

time: 267 us -> 332 us (1.24)
  waiting for transfers between devices: 148 us -> 188 us
  local copies, waits for them, and re-layouts: 27.6 us -> 42.9 us
  starting transfers between devices: 4.62 us -> 16.3 us
    all_to_all x0 -> x1, waiting for transfers between devices: none -> 125 us  [all_by_exchange(): return jnp.concatenate(lax.all_to_all(repeated, axis, 0, 0), axis=dim)]
    all_gather x1 -> x0, waiting for transfers between devices: 56 us -> none  [per_device(): lax.all_gather(values_flat, 'frame', axis=0, tiled=True)]
    all_gather x1, waiting for transfers between devices: 50.5 us -> 0.01 us  [per_device(): lax.all_gather(keys_flat, 'frame', axis=0, tiled=True)]
    another operation x0 -> x2, local copies, waits for them, and re-layouts: none -> 13.9 us  [the longest x1 10.5 us: attend(): value_heads = value_part.reshape(key_span, -1, HD)]
    all_to_all x0 -> x1, starting transfers between devices: none -> 11.7 us  [all_by_exchange(): return jnp.concatenate(lax.all_to_all(repeated, axis, 0, 0), axis=dim)]
    unnamed x4 -> x3, waiting for transfers between devices: 41.9 us -> 52.8 us
    ppermute x1, waiting for transfers between devices: 0.01 us -> 10.2 us  [with_halo(): lax.ppermute(head, axis, [((i + 1) % count, i) for i in range(ends)])]
    all_to_all x0 -> x1, local copies, waits for them, and re-layouts: none -> 9 us  [all_by_exchange(): return jnp.concatenate(lax.all_to_all(repeated, axis, 0, 0), axis=dim)]
  transfers between devices with their start and end apart: 5 -> 5, of which waited for: 3 -> 3; matrix products, arithmetic and copies ran while one was open for 14% -> 16% of each run, Pallas kernels for 0% -> 0%
where the time goes in v1:
time: 332 us; the launch traced here: 331 us
  waiting for transfers between devices  188 us (57%)
  matrix products  45.3 us (14%)
  local copies, waits for them, and re-layouts  42.9 us (13%)
  blocking collectives  17.4 us (5%)
  starting transfers between devices  16.3 us (5%)
  between operations  14.3 us (4%)
  other arithmetic  7.05 us (2%)
    all_to_all x1, waiting for transfers between devices, all_by_exchange(): return jnp.concatenate(lax.all_to_all(repeated, axis, 0, 0), axis=dim)  125 us
    unnamed x3, waiting for transfers between devices  52.8 us
    dot_general x2, matrix products, attend(): jnp.einsum('qhd,khd->hqk', queries, key_heads, preferred_element_type=jnp...  18.1 us
    psum x1, blocking collectives, per_device(): checksum = lax.psum(jnp.sum(full_rows, axis=1) * D ** (-0.5), 'head')  17.4 us
    dot_general x2, matrix products, attend(): jnp.einsum('hqk,khd->qhd', weights.astype(jnp.bfloat16), value_heads, pre...  15.1 us
    all_to_all x1, starting transfers between devices, all_by_exchange(): return jnp.concatenate(lax.all_to_all(repeated, axis, 0, 0), axis=dim)  11.7 us
    another operation x1, local copies, waits for them, and re-layouts, attend(): value_heads = value_part.reshape(key_span, -1, HD)  10.5 us
    ppermute x1, waiting for transfers between devices, with_halo(): lax.ppermute(head, axis, [((i + 1) % count, i) for i in range(ends)])  10.2 us
  transfers between devices with their start and end apart: 5, of which 3 were waited for; matrix products, arithmetic and copies ran while one was open for 16% of the time, Pallas kernels for 0%

profile of v1, /device:TPU:8, one launch (start us, length us, event | category | flops | bytes accessed | tf_op | source)
XLA Modules:
  0.0 331.0 jit_solution(10883477998026256964)
XLA Ops:
  7.2 0.0 copy-start
  7.2 3.3 fusion.27
  10.5 0.1 copy.45
  10.6 3.4 %stack.8 = bf16[32,256,384]{1,2,0:T(8,128)(2,1)} broadcast(bf16[256,384]{0,1:T(8,128)(2,1)S(1)} %copy.45), dimensions={1,2} | broadcast | bytes 6488064 | tf_op jit(solution)/shard_map/stack | solution.py:12
  14.0 11.7 %all-to-all-start = ((bf16[32,256,384]{1,2,0:T(8,128)(2,1)}), bf16[32,256,384]{1,2,0:T(8,128)(2,1)}, u32[]{:S(2)}, u32[]{:S(2)}) async-start(bf16[32,256,384]{1,2,0:T(8,128)(2,1)} %stack.8), calls=%async_computation | async-start | bytes 12582912 | tf_op jit(solution)/shard_map/all_to_all | solution.py:13
  25.7 0.0 all-gather.2.cloned.1.call-start
  25.8 5.0 %slice_bitcast_fusion = (bf16[384,3072]{0,1:T(8,128)(2,1)}, bf16[384,3072]{0,1:T(8,128)(2,1)}) fusion(bf16[3,3072,384]{2,1,0:T(8,128)(2,1)} %param.8), kind=kLoop, calls=%fused_computation.17 | loop fusion | bytes 9437184 | tf_op jit(solution)/shard_map/dot_general | solution.py:94
  30.7 4.3 %copy.38 = bf16[384,3072]{1,0:T(8,128)(2,1)} copy(bf16[384,3072]{0,1:T(8,128)(2,1)} %get-tuple-element.5) | data formatting | bytes 4718592 | tf_op jit(solution)/shard_map/dot_general | solution.py:95
  35.0 3.0 multiply_reduce_fusion.1
  38.0 0.0 copy-done.6
  38.1 0.8 multiply_convert_fusion.1
  38.9 0.0 all-gather.2.cloned.1.call-update
  38.9 0.0 reduce-scatter.4.cloned.1.call-start
  38.9 1.1 copy.39
  40.0 0.8 pad_maximum_fusion.1
  40.8 2.0 collective-permute-start.1
  42.9 2.5 collective-permute-start
  45.4 0.0 copy-start.7
  45.4 0.0 copy-start.8
  45.4 4.3 %copy.41 = bf16[384,3072]{1,0:T(8,128)(2,1)} copy(bf16[384,3072]{0,1:T(8,128)(2,1)} %get-tuple-element.4) | data formatting | bytes 4718592 | tf_op jit(solution)/shard_map/dot_general | solution.py:94
  49.8 0.2 select_reduce_fusion
  50.0 0.4 fusion.7
  50.5 3.8 %fusion.8 = pred[256,8192]{1,0:T(8,128)(4,1)} fusion(s32[8192]{0:T(1024)S(1)} %select_reduce_fusion, s32[8192]{0:T(1024)S(1)} %fusion.35, pred[8192]{0:T(1024)(128)(4,1)S(1)} %iota_compare_fusion.4, pred[2,8192]{1,0:T(4,128)(4,1)S(1)} %fusion.7), kind=kLoop, calls=%fused_computation.10 | loop fusion | flops 10485760 | bytes 2187264 | tf_op jit(solution)/shard_map/and | solution.py:72
  54.4 0.1 select_reduce_fusion.1
  54.5 0.1 fusion.32
  54.6 0.9 fusion.34
  55.5 3.0 multiply_reduce_fusion
  58.6 10.2 %collective-permute-done.1 = bf16[2,256,384]{2,1,0:T(8,128)(2,1)S(1)} collective-permute-done((bf16[2,256,384]{2,1,0:T(8,128)(2,1)}, bf16[2,256,384]{2,1,0:T(8,128)(2,1)S(1)}, u32[]{:S(2)}, u32[]{:S(2)}) %collective-permute-start.1) | collective-permute-done | bytes 393248 | tf_op jit(solution)/shard_map/ppermute | solution.py:26
  68.8 0.0 collective-permute-done
  68.8 0.1 pad_maximum_fusion
  68.9 0.1 fusion.66
  69.1 1.1 copy.40
  70.1 0.3 copy.42
  70.4 3.2 fusion.13
  73.6 124.7 %all-to-all-done = bf16[32,256,384]{1,2,0:T(8,128)(2,1)} async-done(((bf16[32,256,384]{1,2,0:T(8,128)(2,1)}), bf16[32,256,384]{1,2,0:T(8,128)(2,1)}, u32[]{:S(2)}, u32[]{:S(2)}) %all-to-all-start) | async-done | bytes 6291488 | tf_op jit(solution)/shard_map/all_to_all | solution.py:13
  198.3 9.0 %copy.46 = bf16[32,256,384]{1,0,2:T(8,128)(2,1)} copy(bf16[32,256,384]{1,2,0:T(8,128)(2,1)} %all-to-all-done) | data formatting | bytes 12582912 | tf_op jit(solution)/shard_map/all_to_all | solution.py:13
  207.3 10.5 %reshape_reshape.3 = bf16[8192,3,128]{0,2,1:T(8,128)(2,1)} reshape(bf16[32,256,384]{1,0,2:T(8,128)(2,1)} %copy.46) | data formatting | bytes 12582912 | tf_op jit(solution)/shard_map/reshape;reshape | solution.py:77
  217.8 15.0 %fusion = (f32[3,256]{1,0:T(4,128)S(1)}, f32[3,256,8192]{2,1,0:T(8,128)}) fusion(pred[256,8192]{1,0:T(8,128)(4,1)} %fusion.8, bf16[8192,3,128]{0,2,1:T(8,128)(2,1)} %bitcast.81, f32[256,3,128]{0,2,1:T(8,128)S(1)} %copy-done.5, f32[3,128]{1,0:T(4,128)S(1)} %bitcast.79, f32[256,3]{0,1:T(4,128)S(1)} %add_rsqrt_fusion), kind=kOutput, calls=%fused_computation.1 | convolution fusion | flops 1623588096 | bytes 33955328 | tf_op jit(solution)/shard_map/qhd,khd->hqk/dot_general | solution.py:78
  232.8 12.9 %fusion.2 = f32[3,128,256]{2,1,0:T(8,128)S(1)} fusion(bf16[8192,3,128]{0,2,1:T(8,128)(2,1)} %reshape_reshape.3, f32[3,256,8192]{2,1,0:T(8,128)} %get-tuple-element.15, pred[256,8192]{1,0:T(8,128)(4,1)} %fusion.8), kind=kOutput, calls=%fused_computation.3 | convolution fusion | flops 1623195648 | bytes 33947648 | tf_op jit(solution)/shard_map/hqk,khd->qhd/dot_general | solution.py:80
  245.7 2.3 fusion.24
  247.9 2.2 fusion.9
  250.1 2.6 copy.53
  252.7 0.0 reduce-scatter.4.cloned.1.call-update
  252.7 52.8 %reduce-scatter.4.cloned.1.call-done = bf16[384,256]{1,0:T(8,128)(2,1)} async-done(((bf16[3072,256]{1,0:T(8,128)(2,1)}), bf16[384,256]{1,0:T(8,128)(2,1)}) %reduce-scatter.4.cloned.1.call-update) | async-done | bytes 196624
  305.5 1.1 copy.54
  306.6 0.0 copy-start.3
  306.6 0.1 convert_reduce_fusion
  306.7 17.4 %psum.7 = f32[256]{0:T(256)} all-reduce(f32[256]{0:T(256)S(1)} %broadcast_multiply_fusion), channel_id=1, replica_groups=mesh['frame'=32,'head'=8] {'head'}, use_global_device_ids=true, to_apply=%region_8.9 | all-reduce | flops 256 | bytes 2048 | tf_op jit(solution)/shard_map/psum | solution.py:131
  (30 shorter events, 0.2 us)
Async XLA Ops:
  7.2 240.8 %copy-start = (bf16[384,3072]{1,0:T(8,128)(2,1)S(1)}, bf16[384,3072]{1,0:T(8,128)(2,1)}, u32[]{:S(2)}) copy-start(bf16[384,3072]{1,0:T(8,128)(2,1)} %param.10) | copy-start | bytes 7077892
  14.0 184.3 %all-to-all-start = ((bf16[32,256,384]{1,2,0:T(8,128)(2,1)}), bf16[32,256,384]{1,2,0:T(8,128)(2,1)}, u32[]{:S(2)}, u32[]{:S(2)}) async-start(bf16[32,256,384]{1,2,0:T(8,128)(2,1)} %stack.8), calls=%async_computation | async-start | bytes 12582912 | tf_op jit(solution)/shard_map/all_to_all | solution.py:13
  25.7 192.1 %all-gather.2.cloned.1.call-start = ((), (), s32[]{:S(2)}) async-start(), calls=%async_computation.2 | async-start | bytes 6488064 | tf_op jit(solution)/shard_map/all_gather | solution.py:113
  35.0 3.0 copy-start.6
  38.9 266.6 %reduce-scatter.4.cloned.1.call-start = ((), (), s32[]{:S(2)}) async-start(), calls=%async_computation.3 | async-start | bytes 1769472
  40.8 28.0 %collective-permute-start.1 = (bf16[2,256,384]{2,1,0:T(8,128)(2,1)}, bf16[2,256,384]{2,1,0:T(8,128)(2,1)S(1)}, u32[]{:S(2)}, u32[]{:S(2)}) collective-permute-start(bf16[2,256,384]{2,1,0:T(8,128)(2,1)} %pad_maximum_fusion.1), channel_id=1, source_target_pairs={{8,0},{16,8},{24,16},{32,24},{40,32},{48,40},{56,48},{64,56},{72,6... | collective-permute-start | bytes 1179656 | tf_op jit(solution)/shard_map/ppermute | solution.py:26
  42.9 26.0 %collective-permute-start = (bf16[2,256,384]{2,1,0:T(8,128)(2,1)}, bf16[2,256,384]{2,1,0:T(8,128)(2,1)S(1)}, u32[]{:S(2)}, u32[]{:S(2)}) collective-permute-start(bf16[2,256,384]{2,1,0:T(8,128)(2,1)} %pad_maximum_fusion.1), channel_id=1, source_target_pairs={{0,8},{8,16},{16,24},{24,32},{32,40},{40,48},{48,56},{56,64},{64,7... | collective-permute-start | bytes 1179656 | tf_op jit(solution)/shard_map/ppermute | solution.py:24
  45.4 4.4 %copy-start.7 = (s32[32]{0:T(128)S(1)}, s32[32]{0:T(128)}, u32[]{:S(2)}) copy-start(s32[32]{0:T(128)} %param.13) | copy-start | bytes 388
  45.4 4.7 %copy-start.8 = (s32[2,64]{1,0:T(2,128)S(1)}, s32[2,64]{1,0:T(2,128)}, u32[]{:S(2)}) copy-start(s32[2,64]{1,0:T(2,128)} %param.12) | copy-start | bytes 1540
  49.7 4.8 %copy-start.9 = (s32[2,4]{1,0:T(2,128)S(1)}, s32[2,4]{1,0:T(2,128)}, u32[]{:S(2)}) copy-start(s32[2,4]{1,0:T(2,128)} %param.11) | copy-start | bytes 100
  49.7 5.8 %copy-start.1 = (bf16[384,3072]{1,0:T(8,128)(2,1)S(1)}, bf16[384,3072]{1,0:T(8,128)(2,1)}, u32[]{:S(2)}) copy-start(bf16[384,3072]{1,0:T(8,128)(2,1)} %copy.41) | copy-start | bytes 7077892
  207.3 10.5 %copy-start.5 = (f32[256,3,128]{0,2,1:T(8,128)S(1)}, f32[256,3,128]{0,2,1:T(8,128)}, u32[]{:S(2)}) copy-start(f32[256,3,128]{0,2,1:T(8,128)} %get-tuple-element.11) | copy-start | bytes 1179652
  232.8 12.9 %copy-start.2 = (pred[256,768]{1,0:T(8,128)(4,1)S(1)}, pred[256,768]{1,0:T(8,128)(4,1)}, u32[]{:S(2)}) copy-start(pred[256,768]{1,0:T(8,128)(4,1)} %fusion.34) | copy-start | bytes 589828
  232.8 12.9 %copy-start.4 = (bf16[1,768,384]{1,2,0:T(8,128)(2,1)S(1)}, bf16[1,768,384]{1,2,0:T(8,128)(2,1)}, u32[]{:S(2)}) copy-start(bf16[1,768,384]{1,2,0:T(8,128)(2,1)} %copy.40) | copy-start | bytes 1769476
  306.6 17.6 %copy-start.3 = (bf16[384,256]{0,1:T(8,128)(2,1)}, bf16[384,256]{0,1:T(8,128)(2,1)S(1)}, u32[]{:S(2)}) copy-start(bf16[384,256]{0,1:T(8,128)(2,1)S(1)} %copy.54) | copy-start | bytes 589828
Sparse Core Ops, SparseCore 0:
  39.0 151.3 all-gather.1
  252.8 52.6 reduce-scatter.3
